TPU v7x, 256 devices: a whole 4x4x8 slice. The times are simulated.
256 devices in a mesh: row: 32 (over y, z), col: 8 (over x, core).
Axes of the slice: x: 4, y: 4, z: 8, core: 2. Of those that a mesh axis runs over, the one named last changes fastest.
Arguments:
- responses: bfloat16 [4096, 2, 3, 2048], P(('col', 'row')), may hold values from -6 to 6
- labels: int32 [2048], replicated, may hold values from 0 to 15
- conductivity: float32 [16], replicated, may hold values from 0.05 to 2
- permittivity: float32 [16], replicated, may hold values from 0.1 to 1.6
Outputs:
- noise_cov: float32 [2, 4096, 4096], P(None, 'row', 'col')
- energy_gram: float32 [2, 4096, 4096], P(None, 'row', 'col')
All inputs are finite; a program needn't handle non-finite values.
Results may differ from a plain program's by a relative error of at most 0.0021.
Values may be sent and summed in bfloat16 or wider, within the bound.
No kernel may reach another device: no remote copies, remote signals or barrier semaphores. Data moves between devices by JAX's collectives and lax.ppermute only.
A program may use at most 128 MiB of HBM per device.

v0:
```python
import jax
import jax.numpy as jnp
from jax import lax
from jax.sharding import PartitionSpec as P


def broadcast(block, axis, holder):
    block = jnp.where(lax.axis_index(axis) == holder, block, jnp.zeros_like(block))
    return lax.psum(block, axis)


def tile_products(row_fields, right_fields, vox_labels, conductivity, permittivity, scale_factor):
    classes = jnp.arange(conductivity.shape[0], dtype=jnp.int32)
    onehot = (vox_labels[None, :] == classes[:, None]).astype(jnp.float32)
    cond_voxel = jnp.sum(onehot * conductivity[:, None], axis=0) * scale_factor
    perm_voxel = jnp.sum(onehot * permittivity[:, None], axis=0) * scale_factor
    fields = row_fields.astype(jnp.float32)
    vox_here = row_fields.shape[3]
    row_total = row_fields.shape[0]

    def weighted(weight_vec):
        scaled = fields * weight_vec[None, None, None, :]
        crossed = jnp.concatenate([-scaled[:, 1:2], scaled[:, 0:1]], axis=1)
        return (scaled.astype(jnp.bfloat16), crossed.astype(jnp.bfloat16))

    sig_plain, sig_cross = weighted(cond_voxel)
    eps_plain, eps_cross = weighted(perm_voxel)
    left_stack = jnp.concatenate([sig_plain, sig_cross, eps_plain, eps_cross], axis=0)
    left_stack = left_stack.reshape(4 * row_total, 6 * vox_here)
    right_flat = right_fields.reshape(right_fields.shape[0], 6 * vox_here)
    products = lax.dot_general(
        left_stack, right_flat, (((1,), (1,)), ((), ())), preferred_element_type=jnp.float32
    )
    return products.reshape(4, row_total, right_fields.shape[0])


def body(responses, labels, conductivity, permittivity):
    nb_dev = responses.shape[0]
    vox_total = labels.shape[0]
    row_count = lax.axis_size("row")
    col_count = lax.axis_size("col")
    row_block = nb_dev * col_count
    row_index = lax.axis_index("row")
    scale_factor = 1.0 / jnp.sqrt(jnp.float32(6 * vox_total))
    columns = lax.all_gather(responses, "row", axis=0, tiled=True)
    row_ratio = row_count // col_count
    own_rows = lax.dynamic_slice_in_dim(columns, row_index % row_ratio * row_block, row_block, 0)
    row_fields = broadcast(own_rows, "col", row_index // row_ratio)
    products = tile_products(row_fields, columns, labels, conductivity, permittivity, scale_factor)
    noise_cov = products[0:2]
    energy_gram = products[2:4]
    return (noise_cov, energy_gram)


def solution(mesh):
    in_specs = (P(("col", "row"), None, None, None), P(), P(), P())
    out_specs = (P(None, "row", "col"), P(None, "row", "col"))
    return jax.shard_map(body, mesh=mesh, in_specs=in_specs, out_specs=out_specs, check_vma=False)
```

profile of v0, /device:TPU:8, one launch (start us, length us, event | category | flops | bytes accessed | tf_op | source)
XLA Modules:
  0.0 240.6 jit_solution(9226071765441624125)
XLA Ops:
  7.2 0.0 copy-start.4
  7.2 0.0 copy-start.3
  7.2 0.0 copy-start.2
  7.2 0.0 all-gather.2.cloned.1.call-start
  7.2 1.9 copy.7
  9.1 0.0 all-gather.2.cloned.1.call-update
  9.1 0.0 all-reduce.2.cloned.1.call-start
  9.2 123.3 %all-gather.2.cloned.1.call-done = bf16[512,2,3,2048]{3,0,2,1:T(8,128)(2,1)} async-done(((bf16[16,2,3,2048]{3,0,2,1:T(8,128)(2,1)}), bf16[512,2,3,2048]{3,0,2,1:T(8,128)(2,1)}) %all-gather.2.cloned.1.call-update) | async-done | bytes 12582928 | tf_op jit(solution)/shard_map/all_gather | solution.py:45
  132.5 4.5 %dynamic-slice_select_fusion = bf16[128,2,3,2048]{3,0,2,1:T(8,128)(2,1)} fusion(bf16[512,2,3,2048]{3,0,2,1:T(8,128)(2,1)} %all-gather.2.cloned.1.call-done, s32[]{:T(128)S(6)} %select_n.25, pred[]{:T(512)S(6)} %eq.18), kind=kLoop, calls=%fused_computation.18 | loop fusion | flops 1572864 | bytes 6291461 | tf_op jit(solution)/shard_map/jit(_where)/select_n | solution.py:8
  137.0 0.0 all-reduce.2.cloned.1.call-update
  137.0 0.0 copy-done.4
  137.0 0.0 copy-done.3
  137.1 0.0 copy-done.2
  137.1 0.1 select_reduce_fusion.1
  137.2 72.5 %all-reduce.2.cloned.1.call-done = bf16[128,2,3,2048]{3,0,2,1:T(8,128)(2,1)} async-done(((bf16[128,2,3,2048]{3,0,2,1:T(8,128)(2,1)}), bf16[128,2,3,2048]{3,0,2,1:T(8,128)(2,1)}) %all-reduce.2.cloned.1.call-update) | async-done | bytes 3145744 | tf_op jit(solution)/shard_map/psum | solution.py:9
  209.7 6.8 %convert_multiply_fusion.1 = (f32[128,2,3,2048]{3,0,2,1:T(8,128)S(1)}, bf16[128,2,3,2048]{3,0,2,1:T(8,128)(2,1)}, bf16[128,2,3,2048]{3,0,2,1:T(8,128)(2,1)}, f32[128,2,3,2048]{3,0,2,1:T(8,128)S(1)}) fusion(bf16[128,2,3,2048]{3,0,2,1:T(8,128)(2,1)} %all-reduce.2.cloned.1.call-done, f32[2048]{0:T(1024)S(1)} %get-tuple-element.13, f32[2048]{0:T(1024)S(1)} %get-tuple-element.12), kind=kLoop, calls=%fused_computation.13 | loop fusion | flops 7864320 | bytes 22036480 | tf_op jit(solution)/shard_map/mul | solution.py:22
  216.5 0.0 copy-start
  216.5 0.0 copy-start.1
  216.5 0.2 fusion.13
  216.7 0.2 fusion.12
  217.0 1.4 copy-done
  218.4 0.2 slice.35
  218.5 0.8 copy-done.1
  219.3 0.2 slice.37
  219.5 13.2 %fusion.14 = f32[512,512]{1,0:T(8,128)S(1)} fusion(bf16[512,2,3,2048]{3,0,2,1:T(8,128)(2,1)} %all-gather.2.cloned.1.call-done, bf16[128,1,3,2048]{3,0,2,1:T(8,128)(2,1)S(1)} %slice.37, bf16[128,1,3,2048]{3,0,2,1:T(8,128)(2,1)S(1)} %fusion.12, bf16[128,2,3,2048]{3,0,2,1:T(8,128)(2,1)S(1)} %copy-done.1, bf16[128,1,3,2048]{3,0,2,1:T(8,128)(2,1)S(1)} %slice.35, ...), kind=kOutput, calls=%fused_computation.19 | convolution fusion | flops 6517948416 | bytes 26214400 | tf_op jit(solution)/shard_map/dot_general | solution.py:31
  232.7 1.0 fusion.20
  (1 shorter events, 0.0 us)
Async XLA Ops:
  7.2 129.9 %copy-start.4 = (f32[16]{0:T(128)S(1)}, f32[16]{0:T(128)}, u32[]{:S(2)}) copy-start(f32[16]{0:T(128)} %param.7) | copy-start | bytes 196
  7.2 129.9 %copy-start.3 = (f32[16]{0:T(128)S(1)}, f32[16]{0:T(128)}, u32[]{:S(2)}) copy-start(f32[16]{0:T(128)} %param.6) | copy-start | bytes 196
  7.2 129.9 %copy-start.2 = (s32[2048]{0:T(1024)S(1)}, s32[2048]{0:T(1024)}, u32[]{:S(2)}) copy-start(s32[2048]{0:T(1024)} %param.5) | copy-start | bytes 24580
  7.2 125.3 %all-gather.2.cloned.1.call-start = ((), (), s32[]{:S(2)}) async-start(), calls=%async_computation | async-start | bytes 12976128 | tf_op jit(solution)/shard_map/all_gather | solution.py:45
  9.1 200.5 %all-reduce.2.cloned.1.call-start = ((), (), s32[]{:S(2)}) async-start(), calls=%async_computation.1 | async-start | bytes 6291456 | tf_op jit(solution)/shard_map/psum | solution.py:9
  216.5 1.9 copy-start
  216.5 2.8 %copy-start.1 = (bf16[128,2,3,2048]{3,0,2,1:T(8,128)(2,1)S(1)}, bf16[128,2,3,2048]{3,0,2,1:T(8,128)(2,1)}, u32[]{:S(2)}) copy-start(bf16[128,2,3,2048]{3,0,2,1:T(8,128)(2,1)} %get-tuple-element.8) | copy-start | bytes 9437188
Sparse Core Ops, SparseCore 0:
  11.2 121.3 all-gather.1
  137.2 72.4 all-reduce.1
where the time goes:
time: 241 us
  waiting for transfers between devices  196 us (81%)
  between operations  14.2 us (6%)
  matrix products  13.2 us (5%)
  other arithmetic  11.9 us (5%)
  local copies, waits for them, and re-layouts  5.42 us (2%)
    all_gather x1, waiting for transfers between devices, body(): columns = lax.all_gather(responses, 'row', axis=0, tiled=True)  123 us
    psum x1, waiting for transfers between devices, broadcast(): return lax.psum(block, axis)  72.5 us
    dot_general x1, matrix products, tile_products(): lax.dot_general(left_stack, right_flat, (((1,), (1,)), ((), ())), preferr...  13.2 us
    mul x1, other arithmetic, weighted(): scaled = fields * weight_vec[None, None, None, :]  6.83 us
  transfers between devices with their start and end apart: 2, of which 2 were waited for; matrix products, arithmetic and copies ran while one was open for 0% of the time, Pallas kernels for 0%

commit v1 on v0

--- a/solution.py
+++ b/solution.py
@@ -42,7 +42,9 @@
     row_block = nb_dev * col_count
     row_index = lax.axis_index("row")
     scale_factor = 1.0 / jnp.sqrt(jnp.float32(6 * vox_total))
-    columns = lax.all_gather(responses, "row", axis=0, tiled=True)
+    columns = jnp.concatenate(
+        lax.all_to_all(jnp.stack([responses] * lax.axis_size("row")), "row", 0, 0), axis=0
+    )
     row_ratio = row_count // col_count
     own_rows = lax.dynamic_slice_in_dim(columns, row_index % row_ratio * row_block, row_block, 0)
     row_fields = broadcast(own_rows, "col", row_index // row_ratio)

time: 241 us -> 467 us (1.94)
  waiting for transfers between devices: 196 us -> 330 us
  local copies, waits for them, and re-layouts: 5.42 us -> 79.2 us
  starting transfers between devices: 0.08 us -> 11.8 us
  other arithmetic: 11.9 us -> 17.4 us
    all_to_all x0 -> x1, waiting for transfers between devices: none -> 295 us  [body(): lax.all_to_all(jnp.stack([responses] * lax.axis_size('row')), 'row', 0, 0)]
    all_gather x1 -> x0, waiting for transfers between devices: 123 us -> none  [body(): columns = lax.all_gather(responses, 'row', axis=0, tiled=True)]
    psum x1, waiting for transfers between devices: 72.5 us -> 34.7 us  [broadcast(): return lax.psum(block, axis)]
    another operation x0 -> x2, local copies, waits for them, and re-layouts: none -> 35.7 us  [the longest x1 29.6 us: tile_products(): right_flat = right_fields.reshape(right_fields.shape[0], 6 * vox_here)]
    all_to_all x0 -> x2, local copies, waits for them, and re-layouts: none -> 24.3 us  [body(): lax.all_to_all(jnp.stack([responses] * lax.axis_size('row')), 'row', 0, 0)]
    concatenate x0 -> x1, local copies, waits for them, and re-layouts: none -> 16.7 us  [tile_products(): jnp.concatenate([sig_plain, sig_cross, eps_plain, eps_cross], axis=0)]
    all_to_all x0 -> x1, starting transfers between devices: none -> 11.8 us  [body(): lax.all_to_all(jnp.stack([responses] * lax.axis_size('row')), 'row', 0, 0)]
    concatenate x0 -> x1, other arithmetic: none -> 5.58 us  [tile_products(): jnp.concatenate([sig_plain, sig_cross, eps_plain, eps_cross], axis=0)]
  transfers between devices with their start and end apart: 2 -> 2, of which waited for: 2 -> 2; matrix products, arithmetic and copies ran while one was open for 0% -> 10% of each run, Pallas kernels for 0% -> 0%
where the time goes in v1:
time: 467 us; the launch traced here: 466 us
  waiting for transfers between devices  330 us (71%)
  local copies, waits for them, and re-layouts  79.2 us (17%)
  other arithmetic  17.4 us (4%)
  between operations  14.2 us (3%)
  matrix products  13.4 us (3%)
  starting transfers between devices  11.8 us (3%)
    all_to_all x1, waiting for transfers between devices, body(): lax.all_to_all(jnp.stack([responses] * lax.axis_size('row')), 'row', 0, 0)  295 us
    psum x1, waiting for transfers between devices, broadcast(): return lax.psum(block, axis)  34.7 us
    another operation x1, local copies, waits for them, and re-layouts, tile_products(): right_flat = right_fields.reshape(right_fields.shape[0], 6 * vox_here)  29.6 us
    all_to_all x2, local copies, waits for them, and re-layouts, body(): lax.all_to_all(jnp.stack([responses] * lax.axis_size('row')), 'row', 0, 0)  24.3 us
    concatenate x1, local copies, waits for them, and re-layouts, tile_products(): jnp.concatenate([sig_plain, sig_cross, eps_plain, eps_cross], axis=0)  16.7 us
    dot_general x1, matrix products, tile_products(): lax.dot_general(left_stack, right_flat, (((1,), (1,)), ((), ())), preferr...  13.4 us
    all_to_all x1, starting transfers between devices, body(): lax.all_to_all(jnp.stack([responses] * lax.axis_size('row')), 'row', 0, 0)  11.8 us
  transfers between devices with their start and end apart: 2, of which 2 were waited for; matrix products, arithmetic and copies ran while one was open for 10% of the time, Pallas kernels for 0%

profile of v1, /device:TPU:8, one launch (start us, length us, event | category | flops | bytes accessed | tf_op | source)
XLA Modules:
  0.0 465.5 jit_solution(7724721392845449087)
XLA Ops:
  7.2 1.1 copy.16
  8.3 6.1 %stack.2 = bf16[32,16,2,3,2048]{4,1,3,2,0:T(8,128)(2,1)} broadcast(bf16[16,2,3,2048]{3,0,2,1:T(8,128)(2,1)S(1)} %copy.16), dimensions={1,2,3,4} | broadcast | bytes 12976128 | tf_op jit(solution)/shard_map/stack | solution.py:46
  14.4 11.8 %all-to-all-start = ((bf16[32,16,2,3,2048]{4,1,3,2,0:T(8,128)(2,1)}), bf16[32,16,2,3,2048]{4,1,3,2,0:T(8,128)(2,1)}, u32[]{:S(2)}, u32[]{:S(2)}) async-start(bf16[32,16,2,3,2048]{4,1,3,2,0:T(8,128)(2,1)} %stack.2), calls=%async_computation | async-start | bytes 25165824 | tf_op jit(solution)/shard_map/all_to_all | solution.py:46
  26.1 0.0 all-reduce.2.cloned.1.call-start
  26.2 294.8 %all-to-all-done = bf16[32,16,2,3,2048]{4,1,3,2,0:T(8,128)(2,1)} async-done(((bf16[32,16,2,3,2048]{4,1,3,2,0:T(8,128)(2,1)}), bf16[32,16,2,3,2048]{4,1,3,2,0:T(8,128)(2,1)}, u32[]{:S(2)}, u32[]{:S(2)}) %all-to-all-start) | async-done | bytes 12582944 | tf_op jit(solution)/shard_map/all_to_all | solution.py:46
  321.0 6.5 %copy.17 = bf16[32,16,2,3,2048]{4,1,0,3,2:T(8,128)(2,1)S(1)} copy(bf16[32,16,2,3,2048]{4,1,3,2,0:T(8,128)(2,1)} %all-to-all-done) | data formatting | bytes 25165824 | tf_op jit(solution)/shard_map/all_to_all | solution.py:46
  327.5 0.0 copy-start
  327.5 0.0 copy-start.1
  327.5 0.0 copy-start.2
  327.5 2.6 dynamic-slice_select_fusion
  330.1 0.0 all-reduce.2.cloned.1.call-update
  330.1 0.0 copy-done
  330.1 0.0 copy-done.1
  330.1 0.0 copy-done.2
  330.1 0.1 select_reduce_fusion.1
  330.3 17.8 %copy.19 = bf16[32,16,2,3,2048]{4,3,2,1,0:T(4,128)(2,1)} copy(bf16[32,16,2,3,2048]{4,1,3,2,0:T(8,128)(2,1)} %all-to-all-done) | data formatting | bytes 25165824 | tf_op jit(solution)/shard_map/all_to_all | solution.py:46
  348.0 29.6 %reshape_reshape.3 = bf16[512,12288]{1,0:T(8,128)(2,1)} reshape(bf16[32,16,2,3,2048]{4,3,2,1,0:T(4,128)(2,1)} %copy.19) | data formatting | bytes 25165824 | tf_op jit(solution)/shard_map/reshape;reshape | solution.py:30
  377.7 34.7 %all-reduce.2.cloned.1.call-done = bf16[128,2,3,2048]{3,0,2,1:T(8,128)(2,1)} async-done(((bf16[128,2,3,2048]{3,0,2,1:T(8,128)(2,1)}), bf16[128,2,3,2048]{3,0,2,1:T(8,128)(2,1)}) %all-reduce.2.cloned.1.call-update) | async-done | bytes 3145744 | tf_op jit(solution)/shard_map/psum | solution.py:9
  412.4 6.8 %convert_multiply_fusion.1 = (f32[128,2,3,2048]{3,0,2,1:T(8,128)}, bf16[128,2,3,2048]{3,0,2,1:T(8,128)(2,1)S(1)}, bf16[128,2,3,2048]{3,0,2,1:T(8,128)(2,1)S(1)}, f32[128,2,3,2048]{3,0,2,1:T(8,128)S(1)}) fusion(bf16[128,2,3,2048]{3,0,2,1:T(8,128)(2,1)} %all-reduce.2.cloned.1.call-done, f32[2048]{0:T(1024)S(1)} %get-tuple-element.13, f32[2048]{0:T(1024)S(1)} %get-tuple-element.12), kind=kLoop, calls=%fused_computation.2 | loop fusion | flops 7864320 | bytes 22036480 | tf_op jit(solution)/shard_map/mul | solution.py:22
  419.2 2.1 fusion.1
  421.3 0.2 fusion
  421.6 0.2 slice.35
  421.8 0.2 slice.37
  422.0 5.6 %maximum_maximum_fusion = bf16[512,2,3,2048]{3,0,2,1:T(8,128)(2,1)} fusion(bf16[128,1,3,2048]{3,0,2,1:T(8,128)(2,1)S(1)} %slice.37, bf16[128,1,3,2048]{3,0,2,1:T(8,128)(2,1)S(1)} %fusion, bf16[128,2,3,2048]{3,0,2,1:T(8,128)(2,1)S(1)} %get-tuple-element.8, bf16[128,1,3,2048]{3,0,2,1:T(8,128)(2,1)S(1)} %slice.35, bf16[128,1,3,2048]{3,0,2,1:T(8,128)(2,1)S(1)} %fusion.1, ...), kind=kLoop, calls=%fused_computation | loop fusion | flops 75497472 | bytes 25165824 | tf_op jit(solution)/shard_map/concatenate | solution.py:28
  427.5 16.7 %copy.18 = bf16[512,2,3,2048]{0,3,2,1:T(8,128)(2,1)} copy(bf16[512,2,3,2048]{3,0,2,1:T(8,128)(2,1)} %maximum_maximum_fusion) | data formatting | bytes 25165824 | tf_op jit(solution)/shard_map/concatenate | solution.py:28
  444.2 13.4 %fusion.5 = f32[512,512]{1,0:T(8,128)S(1)} fusion(bf16[512,12288]{0,1:T(8,128)(2,1)} %bitcast.7, bf16[512,12288]{1,0:T(8,128)(2,1)} %reshape_reshape.3), kind=kOutput, calls=%fused_computation.16 | convolution fusion | flops 6442450944 | bytes 26214400 | tf_op jit(solution)/shard_map/dot_general | solution.py:31
  457.6 1.0 fusion.4
  (1 shorter events, 0.0 us)
Async XLA Ops:
  14.4 306.6 %all-to-all-start = ((bf16[32,16,2,3,2048]{4,1,3,2,0:T(8,128)(2,1)}), bf16[32,16,2,3,2048]{4,1,3,2,0:T(8,128)(2,1)}, u32[]{:S(2)}, u32[]{:S(2)}) async-start(bf16[32,16,2,3,2048]{4,1,3,2,0:T(8,128)(2,1)} %stack.2), calls=%async_computation | async-start | bytes 25165824 | tf_op jit(solution)/shard_map/all_to_all | solution.py:46
  26.1 386.3 %all-reduce.2.cloned.1.call-start = ((), (), s32[]{:S(2)}) async-start(), calls=%async_computation.1 | async-start | bytes 6291456 | tf_op jit(solution)/shard_map/psum | solution.py:9
  327.5 2.6 copy-start
  327.5 2.6 copy-start.1
  327.5 2.6 copy-start.2
Sparse Core Ops, SparseCore 0:
  330.2 82.1 all-reduce.1

commit v2 on v0

--- a/solution.py
+++ b/solution.py
@@ -6,7 +6,7 @@
 
 def broadcast(block, axis, holder):
     block = jnp.where(lax.axis_index(axis) == holder, block, jnp.zeros_like(block))
-    return lax.psum(block, axis)
+    return jnp.sum(lax.all_gather(block, axis), axis=0)
 
 
 def tile_products(row_fields, right_fields, vox_labels, conductivity, permittivity, scale_factor):

time: 241 us -> 307 us (1.27)
  waiting for transfers between devices: 196 us -> 245 us
  other arithmetic: 11.9 us -> 27.4 us
    all_gather x0 -> x1, waiting for transfers between devices: none -> 121 us  [broadcast(): return jnp.sum(lax.all_gather(block, axis), axis=0)]
    psum x1 -> x0, waiting for transfers between devices: 72.5 us -> none  [broadcast(): return lax.psum(block, axis)]
    reduce_sum x0 -> x1, other arithmetic: none -> 15.6 us  [broadcast(): return jnp.sum(lax.all_gather(block, axis), axis=0)]
where the time goes in v2:
time: 307 us; the launch traced here: 305 us
  waiting for transfers between devices  245 us (80%)
  other arithmetic  27.4 us (9%)
  between operations  14.2 us (5%)
  matrix products  13.2 us (4%)
  local copies, waits for them, and re-layouts  5.42 us (2%)
    all_gather x1, waiting for transfers between devices, body(): columns = lax.all_gather(responses, 'row', axis=0, tiled=True)  123 us
    all_gather x1, waiting for transfers between devices, broadcast(): return jnp.sum(lax.all_gather(block, axis), axis=0)  121 us
    reduce_sum x1, other arithmetic, broadcast(): return jnp.sum(lax.all_gather(block, axis), axis=0)  15.6 us
    dot_general x1, matrix products, tile_products(): lax.dot_general(left_stack, right_flat, (((1,), (1,)), ((), ())), preferr...  13.2 us
    mul x1, other arithmetic, weighted(): scaled = fields * weight_vec[None, None, None, :]  6.79 us
  transfers between devices with their start and end apart: 2, of which 2 were waited for; matrix products, arithmetic and copies ran while one was open for 0% of the time, Pallas kernels for 0%

profile of v2, /device:TPU:8, one launch (start us, length us, event | category | flops | bytes accessed | tf_op | source)
XLA Modules:
  0.0 304.8 jit_solution(16163563384479206754)
XLA Ops:
  7.2 0.0 copy-start.2
  7.2 0.0 copy-start.3
  7.2 0.0 copy-start.4
  7.2 0.0 all-gather.4.cloned.1.call-start
  7.2 1.9 copy.7
  9.1 0.0 all-gather.4.cloned.1.call-update
  9.1 0.0 all-gather.6.cloned.1.call-start
  9.2 123.3 %all-gather.4.cloned.1.call-done = bf16[512,2,3,2048]{3,0,2,1:T(8,128)(2,1)} async-done(((bf16[16,2,3,2048]{3,0,2,1:T(8,128)(2,1)}), bf16[512,2,3,2048]{3,0,2,1:T(8,128)(2,1)}) %all-gather.4.cloned.1.call-update) | async-done | bytes 12582928 | tf_op jit(solution)/shard_map/all_gather | solution.py:45
  132.5 4.4 %dynamic-slice_select_fusion = bf16[128,2,3,2048]{3,0,2,1:T(8,128)(2,1)} fusion(bf16[512,2,3,2048]{3,0,2,1:T(8,128)(2,1)} %all-gather.4.cloned.1.call-done, s32[]{:T(128)S(6)} %select_n.25, pred[]{:T(512)S(6)} %eq.18), kind=kLoop, calls=%fused_computation.18 | loop fusion | flops 1572864 | bytes 6291461 | tf_op jit(solution)/shard_map/jit(_where)/select_n | solution.py:8
  137.0 0.0 all-gather.6.cloned.1.call-update
  137.0 0.0 copy-done.2
  137.0 0.0 copy-done.3
  137.0 0.0 copy-done.4
  137.0 0.1 select_reduce_fusion.1
  137.2 121.1 %all-gather.6.cloned.1.call-done = bf16[1024,2,3,2048]{3,0,2,1:T(8,128)(2,1)} async-done(((bf16[128,2,3,2048]{3,0,2,1:T(8,128)(2,1)}), bf16[1024,2,3,2048]{3,0,2,1:T(8,128)(2,1)}) %all-gather.6.cloned.1.call-update) | async-done | bytes 25165840 | tf_op jit(solution)/shard_map/all_gather | solution.py:9
  258.3 15.6 %reduce_sum.30 = bf16[128,2,3,2048]{3,0,2,1:T(8,128)(2,1)} reduce(bf16[8,128,2,3,2048]{4,1,0,3,2:T(8,128)(2,1)} %bitcast.8, bf16[]{:T(256)} %constant.46.clone.1), dimensions={0}, to_apply=%region_0.1 | reduce | flops 11010048 | bytes 28311554 | tf_op jit(solution)/shard_map/reduce_sum | solution.py:9
  273.9 6.8 %convert_multiply_fusion.1 = (f32[128,2,3,2048]{3,0,2,1:T(8,128)S(1)}, bf16[128,2,3,2048]{3,0,2,1:T(8,128)(2,1)}, bf16[128,2,3,2048]{3,0,2,1:T(8,128)(2,1)}, f32[128,2,3,2048]{3,0,2,1:T(8,128)S(1)}) fusion(bf16[128,2,3,2048]{3,0,2,1:T(8,128)(2,1)} %reduce_sum.30, f32[2048]{0:T(1024)S(1)} %get-tuple-element.13, f32[2048]{0:T(1024)S(1)} %get-tuple-element.12), kind=kLoop, calls=%fused_computation.13 | loop fusion | flops 7864320 | bytes 22036480 | tf_op jit(solution)/shard_map/mul | solution.py:22
  280.7 0.0 copy-start
  280.7 0.0 copy-start.1
  280.7 0.2 fusion.12
  280.9 0.2 fusion.13
  281.2 1.4 copy-done
  282.6 0.2 slice.35
  282.8 0.8 copy-done.1
  283.5 0.2 slice.37
  283.7 13.2 %fusion.14 = f32[512,512]{1,0:T(8,128)S(1)} fusion(bf16[512,2,3,2048]{3,0,2,1:T(8,128)(2,1)} %all-gather.4.cloned.1.call-done, bf16[128,1,3,2048]{3,0,2,1:T(8,128)(2,1)S(1)} %slice.37, bf16[128,1,3,2048]{3,0,2,1:T(8,128)(2,1)S(1)} %fusion.12, bf16[128,2,3,2048]{3,0,2,1:T(8,128)(2,1)S(1)} %copy-done.1, bf16[128,1,3,2048]{3,0,2,1:T(8,128)(2,1)S(1)} %slice.35, ...), kind=kOutput, calls=%fused_computation.19 | convolution fusion | flops 6517948416 | bytes 26214400 | tf_op jit(solution)/shard_map/dot_general | solution.py:31
  296.9 1.0 fusion.20
  (1 shorter events, 0.0 us)
Async XLA Ops:
  7.2 129.8 %copy-start.2 = (s32[2048]{0:T(1024)S(1)}, s32[2048]{0:T(1024)}, u32[]{:S(2)}) copy-start(s32[2048]{0:T(1024)} %param.5) | copy-start | bytes 24580
  7.2 129.8 %copy-start.3 = (f32[16]{0:T(128)S(1)}, f32[16]{0:T(128)}, u32[]{:S(2)}) copy-start(f32[16]{0:T(128)} %param.6) | copy-start | bytes 196
  7.2 129.8 %copy-start.4 = (f32[16]{0:T(128)S(1)}, f32[16]{0:T(128)}, u32[]{:S(2)}) copy-start(f32[16]{0:T(128)} %param.7) | copy-start | bytes 196
  7.2 125.3 %all-gather.4.cloned.1.call-start = ((), (), s32[]{:S(2)}) async-start(), calls=%async_computation | async-start | bytes 12976128 | tf_op jit(solution)/shard_map/all_gather | solution.py:45
  9.1 249.2 %all-gather.6.cloned.1.call-start = ((), (), s32[]{:S(2)}) async-start(), calls=%async_computation.1 | async-start | bytes 28311552 | tf_op jit(solution)/shard_map/all_gather | solution.py:9
  280.7 1.9 copy-start
  280.7 2.8 copy-start.1
Sparse Core Ops, SparseCore 0:
  11.2 121.3 all-gather.3
  137.1 121.1 all-gather.5
